TPU v7x, 256 devices: a whole 4x4x8 slice. The times are simulated.
256 devices in a mesh: expert: 8 (over y, core), shard: 32 (over z, x).
Axes of the slice: x: 4, y: 4, z: 8, core: 2. Of those that a mesh axis runs over, the one named last changes fastest.
Arguments:
- activations: bfloat16 [8, 32, 96, 2048], P('expert', 'shard'), may hold values from -6 to 6
- out_grads: bfloat16 [8, 32, 96, 7168], P('expert', 'shard'), may hold values from -6 to 6
- next_inputs: bfloat16 [8, 32, 96, 2048], P('expert', 'shard'), may hold values from -6 to 6
- counts: int32 [8, 32], P('expert', 'shard'), may hold values from 1 to 96, as said below
- master: float32 [8, 32, 512, 896], P('expert', 'shard'), may hold values from -0.125 to 0.125
- moment: bfloat16 [8, 32, 512, 896], P('expert', 'shard'), may hold values from -6 to 6
- second: bfloat16 [8, 32, 512, 896], P('expert', 'shard'), may hold values from 0.099609375 to 4
Outputs:
- master_new: float32 [8, 32, 512, 896], P('expert', 'shard')
- moment_new: bfloat16 [8, 32, 512, 896], P('expert', 'shard')
- second_new: bfloat16 [8, 32, 512, 896], P('expert', 'shard')
- projected: bfloat16 [8, 32, 96, 7168], P('expert', 'shard')
Inputs may be any that keep to these rules, and one draw needn't show every extreme that they name: counts[e, s] of the 96 slots of expert e from shard s hold tokens, the leading ones; the rest are padding.
All inputs are finite; a program needn't handle non-finite values.
Results may differ from a plain program's by a relative error of at most 0.00055.
The roundings to bfloat16 on the way count: a program that leaves them out, or rounds other values in their place, can miss the bound.
Values may be sent and summed in bfloat16 or wider, within the bound.
No kernel may reach another device: no remote copies, remote signals or barrier semaphores. Data moves between devices by JAX's collectives and lax.ppermute only.
A program may use at most 192 MiB of HBM per device.

v0:
```python
import functools
import jax
import jax.numpy as jnp
from jax import lax
from jax.sharding import Mesh
from jax.sharding import PartitionSpec as P

D = 2048
FF = 7168
SHARD = ("shard_0", "shard_1")
EXPERT = ("expert_0", "expert_1")
EXPERT_SHARD = ("expert_0", "expert_1", "shard_0", "shard_1")


def sent_together(arrays, axis, split_dim, concat_dim, along):
    both = jnp.concatenate(arrays, axis=along)
    filled, at, done = (
        lax.all_to_all(both, axis, split_axis=split_dim, concat_axis=concat_dim, tiled=True),
        0,
        [],
    )
    for a in arrays:
        done.append(lax.slice_in_dim(filled, at, at + a.shape[along], axis=along))
        at += a.shape[along]
    return tuple(done)


def over_axes(shard, axes):
    return functools.reduce(lax.psum, axes, shard)


def from_everyone(shard, axis):
    size = lax.axis_size(axis)
    return lax.all_to_all(
        jnp.broadcast_to(shard[None], (size, *shard.shape)), axis, 0, 0, tiled=True
    )


def over_copies(shard, axis):
    everything = from_everyone(shard, axis)
    return jnp.sum(everything, axis=0)


def together(arrays, axis):
    ends = [0]
    for a in arrays:
        ends.append(ends[-1] + a.size)
    subtotal = over_copies(jnp.concatenate([a.ravel() for a in arrays]), axis)
    return tuple((subtotal[b:e].reshape(a.shape) for a, b, e in zip(arrays, ends, ends[1:])))


def spread_rows(matrix, grid_r, grid_c, stride):
    capacity = matrix.shape[0]
    blocks = matrix.reshape(capacity, grid_r, stride).transpose(1, 0, 2)
    blocks = jnp.broadcast_to(blocks[:, None], (grid_r, grid_c, capacity, stride))
    return blocks.reshape(grid_r * grid_c, capacity, stride)


def spread_cols(matrix, grid_r, grid_c, stride):
    capacity = matrix.shape[0]
    blocks = matrix.reshape(capacity, grid_c, stride).transpose(1, 0, 2)
    blocks = jnp.broadcast_to(blocks[None], (grid_r, grid_c, capacity, stride))
    return blocks.reshape(grid_r * grid_c, capacity, stride)


def body(activations, out_grads, next_inputs, counts, master, moment, second):
    capacity = activations.shape[2]
    d_blk = master.shape[2]
    f_blk = master.shape[3]
    grid_r = D // d_blk
    grid_c = FF // f_blk
    valid = lax.iota(jnp.int32, capacity) < counts[0, 0]
    masked = jnp.where(valid[:, None], out_grads[0, 0], jnp.zeros((), jnp.bfloat16))
    send_rows = spread_rows(activations[0, 0], grid_r, grid_c, d_blk)
    send_cols = spread_cols(masked, grid_r, grid_c, f_blk)
    got_rows, got_cols = sent_together((send_rows, send_cols), SHARD, 0, 0, 2)
    gradient = jnp.einsum("sci,scj->ij", got_rows, got_cols, preferred_element_type=jnp.float32)
    weights = master[0, 0]
    first = moment[0, 0].astype(jnp.float32)
    later = second[0, 0].astype(jnp.float32)
    experts = lax.axis_size(EXPERT) * master.shape[0]
    entries = float(experts * D * FF)
    grad_sq = jnp.sum(gradient * gradient)
    weight_local = jnp.sum(weights * weights)
    norm_total = over_axes(grad_sq, EXPERT_SHARD)
    grad_rms = jnp.sqrt(norm_total / entries + 1e-06)
    clip_factor = jnp.minimum(1.0, 1.0 / grad_rms)
    clipped = clip_factor * gradient
    first_new = 0.9 * first + 0.1 * clipped
    later_new = 0.999 * later + 0.001 * clipped * clipped
    update = (
        first_new / (1.0 - 0.9**10) / (jnp.sqrt(later_new / (1.0 - 0.999**10)) + 1e-06)
        + 0.01 * weights
    )
    update_local = jnp.sum(update * update)
    weight_sq, update_sq = together((weight_local, update_local), SHARD)
    trust_ratio = jnp.sqrt(weight_sq) / (jnp.sqrt(update_sq) + 1e-06)
    weights_new = weights - 0.08 * trust_ratio * update
    rounded = weights_new.astype(jnp.bfloat16)
    inputs_next = next_inputs[0, 0]
    empty = jnp.zeros((capacity, FF), jnp.float32)
    pieces = lax.all_gather(rounded[None], SHARD, axis=0, tiled=True)

    def add_one(tile_index, current):
        tile = lax.dynamic_index_in_dim(pieces, tile_index, 0, keepdims=False)
        row_start = tile_index // grid_c * d_blk
        col_start = tile_index % grid_c * f_blk
        columns = lax.dynamic_slice_in_dim(inputs_next, row_start, d_blk, 1)
        partial_value = jnp.dot(columns, tile, preferred_element_type=jnp.float32)
        before = lax.dynamic_slice_in_dim(current, col_start, f_blk, 1)
        return lax.dynamic_update_slice_in_dim(current, before + partial_value, col_start, 1)

    summed = lax.fori_loop(0, pieces.shape[0], add_one, empty)
    projected = summed.astype(jnp.bfloat16)
    moment_out = first_new.astype(jnp.bfloat16)
    second_out = later_new.astype(jnp.bfloat16)
    return (
        weights_new[None, None],
        moment_out[None, None],
        second_out[None, None],
        projected[None, None],
    )


def solution(mesh):
    finer = Mesh(mesh.devices.reshape(4, 2, 8, 4), ("expert_0", "expert_1", "shard_0", "shard_1"))
    placed = (
        P(EXPERT, SHARD, None, None),
        P(EXPERT, SHARD, None, None),
        P(EXPERT, SHARD, None, None),
        P(EXPERT, SHARD),
        P(EXPERT, SHARD, None, None),
        P(EXPERT, SHARD, None, None),
        P(EXPERT, SHARD, None, None),
    )
    return jax.shard_map(
        body,
        mesh=finer,
        in_specs=placed,
        out_specs=(
            P(EXPERT, SHARD, None, None),
            P(EXPERT, SHARD, None, None),
            P(EXPERT, SHARD, None, None),
            P(EXPERT, SHARD, None, None),
        ),
        check_vma=False,
    )
```

profile of v0, /device:TPU:1, one launch (start us, length us, event | category | flops | bytes accessed | tf_op | source)
XLA Modules:
  0.0 558.3 jit_solution(14726423744017282262)
XLA Ops:
  7.2 1.6 copy.21
  11.1 3.0 broadcast_in_dim.52
  14.4 6.6 %pad_maximum_fusion = bf16[32,96,1408]{2,1,0:T(8,128)(2,1)} fusion(bf16[32,96,896]{2,1,0:T(8,128)(2,1)} %bitcast.80, bf16[32,96,512]{2,1,0:T(8,128)(2,1)S(1)} %bitcast.81), kind=kLoop, calls=%fused_computation.6 | loop fusion | flops 17301504 | bytes 17301504 | tf_op jit(solution)/shard_map/concatenate | solution.py:16
  21.0 203.0 %all_to_all.11 = bf16[32,96,1408]{2,1,0:T(8,128)(2,1)S(1)} all-to-all(bf16[32,96,1408]{2,1,0:T(8,128)(2,1)} %pad_maximum_fusion), channel_id=1, replica_groups=mesh['expert_0'=4,'expert_1'=2,'shard_0'=8,'shard_1'=4] {'shard_0','shar..., dimensions={0} | all-to-all | bytes 17301504 | tf_op jit(solution)/shard_map/all_to_all | solution.py:18
  224.0 5.3 fusion.9
  229.2 9.3 %psum.28 = f32[]{:T(128)} all-reduce(f32[]{:T(128)} %get-tuple-element.135), channel_id=1, replica_groups=mesh['expert_0'=4,'expert_1'=2,'shard_0'=8,'shard_1'=4] {'expert_0'}, use_global_device_ids=true, to_apply=%region_2.3 | all-reduce | flops 1 | bytes 8 | tf_op jit(solution)/shard_map/psum | solution.py:29
  238.5 7.1 %psum.29 = f32[]{:T(128)} all-reduce(f32[]{:T(128)} %psum.28), channel_id=1, replica_groups=mesh['expert_0'=4,'expert_1'=2,'shard_0'=8,'shard_1'=4] {'expert_1'}, use_global_device_ids=true, to_apply=%region_3.4 | all-reduce | flops 1 | bytes 8 | tf_op jit(solution)/shard_map/psum | solution.py:29
  245.7 12.3 %psum.30 = f32[]{:T(128)} all-reduce(f32[]{:T(128)} %psum.29), channel_id=1, replica_groups=mesh['expert_0'=4,'expert_1'=2,'shard_0'=8,'shard_1'=4] {'shard_0'}, use_global_device_ids=true, to_apply=%region_4.5 | all-reduce | flops 1 | bytes 8 | tf_op jit(solution)/shard_map/psum | solution.py:29
  257.9 7.4 %psum.31 = f32[]{:T(128)} all-reduce(f32[]{:T(128)} %psum.30), channel_id=1, replica_groups=mesh['expert_0'=4,'expert_1'=2,'shard_0'=8,'shard_1'=4] {'shard_1'}, use_global_device_ids=true, to_apply=%region_5.6 | all-reduce | flops 1 | bytes 8 | tf_op jit(solution)/shard_map/psum | solution.py:29
  266.1 5.8 %multiply_reduce_fusion = (f32[]{:T(128)}, f32[512,896]{1,0:T(8,128)}, bf16[1,1,512,896]{3,2,1,0:T(8,128)(2,1)}, bf16[1,1,512,896]{3,2,1,0:T(8,128)(2,1)}, f32[]{:T(128)}) fusion(f32[1,1,512,896]{3,2,1,0:T(8,128)S(1)} %copy-done, bf16[1,1,512,896]{3,2,1,0:T(8,128)(2,1)S(1)} %copy-done.1, f32[512,896,1]{1,0,2:T(8,128)} %get-tuple-element.136, f32[]{:T(128)S(6)} %min.3, ...), kind=kLoop, calls=%fused_computation.21 | loop fusion | flops 10092542 | bytes 9175052 | tf_op jit(solution)/shard_map/reduce_sum | solution.py:95
  273.3 13.2 %all_to_all.12 = f32[32,1,2]{2,1,0:T(1,128)S(1)} all-to-all(f32[32,1,2]{2,1,0:T(1,128)S(1)} %broadcast_in_dim.53), channel_id=1, replica_groups=mesh['expert_0'=4,'expert_1'=2,'shard_0'=8,'shard_1'=4] {'shard_0','shar..., dimensions={0} | all-to-all | bytes 512 | tf_op jit(solution)/shard_map/all_to_all | solution.py:34
  288.6 3.3 fusion.14
  291.9 207.4 %all-gather.3.cloned.1.call-done = bf16[16384,896]{1,0:T(8,128)(2,1)} async-done(((bf16[512,896]{1,0:T(8,128)(2,1)}), bf16[16384,896]{1,0:T(8,128)(2,1)}) %all-gather.3.cloned.1.call-update) | async-done | bytes 29360144 | tf_op jit(solution)/shard_map/all_gather | solution.py:102
  499.5 50.7 %while.15 = (s32[]{:T(128)}, f32[96,7168]{1,0:T(8,128)S(1)}, bf16[96,2048]{1,0:T(8,128)(2,1)}, bf16[32,512,896]{2,1,0:T(8,128)(2,1)}, s32[]{:T(128)}, /*index=5*...) while((s32[]{:T(128)}, f32[96,7168]{1,0:T(8,128)S(1)}, ...), condition=%wide.region_9.10_spmd, body=%wide.region_8.9_spmd.sunk | while | flops 88166424 | bytes 1704796 | solution.py:113
  504.3 1.5 fusion.23
  515.4 1.5 fusion.23
  517.0 1.5 fusion.23
  523.3 1.5 fusion.23
  526.5 1.5 fusion.23
  529.6 1.5 fusion.23
  535.9 1.5 fusion.23
  540.7 1.5 fusion.23
  542.3 1.5 fusion.23
  548.6 1.5 fusion.23
  (42 shorter events, 39.5 us)
Async XLA Ops:
  7.2 492.1 %all-gather.3.cloned.1.call-start = ((), (), s32[]{:S(2)}) async-start(), calls=%async_computation.2 | async-start | bytes 30277632 | tf_op jit(solution)/shard_map/all_gather | solution.py:102
  9.7 1.0 copy-start.2
  223.9 42.1 %copy-start = (f32[1,1,512,896]{3,2,1,0:T(8,128)S(1)}, f32[1,1,512,896]{3,2,1,0:T(8,128)}, u32[]{:S(2)}) copy-start(f32[1,1,512,896]{3,2,1,0:T(8,128)} %param.13) | copy-start | bytes 5505028
  223.9 42.1 %copy-start.1 = (bf16[1,1,512,896]{3,2,1,0:T(8,128)(2,1)S(1)}, bf16[1,1,512,896]{3,2,1,0:T(8,128)(2,1)}, u32[]{:S(2)}) copy-start(bf16[1,1,512,896]{3,2,1,0:T(8,128)(2,1)} %param.15) | copy-start | bytes 2752516
Sparse Core Ops, SparseCore 0:
  292.0 207.2 all-gather.2
where the time goes:
time: 560 us; the launch traced here: 558 us
  blocking collectives  252 us (45%)
  waiting for transfers between devices  207 us (37%)
  matrix products  54.7 us (10%)
  other arithmetic  18.6 us (3%)
  between operations  16.9 us (3%)
  local copies, waits for them, and re-layouts  7.05 us (1%)
    all_gather x1, waiting for transfers between devices, body(): pieces = lax.all_gather(rounded[None], SHARD, axis=0, tiled=True)  207 us
    all_to_all x1, blocking collectives, sent_together(): lax.all_to_all(both, axis, split_axis=split_dim, concat_axis=concat_dim,...  203 us
    dot_general x32, matrix products, add_one(): partial_value = jnp.dot(columns, tile, preferred_element_type=jnp.float32)  49.4 us
    psum x4, blocking collectives, over_axes(): return functools.reduce(lax.psum, axes, shard)  36.1 us
    all_to_all x1, blocking collectives, from_everyone(): lax.all_to_all(jnp.broadcast_to(shard[None], (size, *shard.shape)), axis,...  13.2 us
  transfers between devices with their start and end apart: 1, of which 1 were waited for; matrix products, arithmetic and copies ran while one was open for 0% of the time, Pallas kernels for 0%

commit v1 on v0

--- a/solution.py
+++ b/solution.py
@@ -99,7 +99,9 @@
     rounded = weights_new.astype(jnp.bfloat16)
     inputs_next = next_inputs[0, 0]
     empty = jnp.zeros((capacity, FF), jnp.float32)
-    pieces = lax.all_gather(rounded[None], SHARD, axis=0, tiled=True)
+    pieces = jnp.concatenate(
+        lax.all_to_all(jnp.stack([rounded[None]] * lax.axis_size(SHARD)), SHARD, 0, 0), axis=0
+    )
 
     def add_one(tile_index, current):
         tile = lax.dynamic_index_in_dim(pieces, tile_index, 0, keepdims=False)

time: 560 us -> 1040 us (1.86)
  waiting for transfers between devices: 207 us -> 690 us
  between operations: 16.9 us -> 3.55 us
    all_to_all x0 -> x1, waiting for transfers between devices: none -> 690 us  [body(): lax.all_to_all(jnp.stack([rounded[None]] * lax.axis_size(SHARD)), SHARD,...]
    all_gather x1 -> x0, waiting for transfers between devices: 207 us -> none  [body(): pieces = lax.all_gather(rounded[None], SHARD, axis=0, tiled=True)]
where the time goes in v1:
time: 1040 us
  waiting for transfers between devices  690 us (66%)
  blocking collectives  252 us (24%)
  matrix products  54.7 us (5%)
  other arithmetic  18.3 us (2%)
  local copies, waits for them, and re-layouts  17.3 us (2%)
    all_to_all x1, waiting for transfers between devices, body(): lax.all_to_all(jnp.stack([rounded[None]] * lax.axis_size(SHARD)), SHARD,...  690 us
    all_to_all x1, blocking collectives, sent_together(): lax.all_to_all(both, axis, split_axis=split_dim, concat_axis=concat_dim,...  203 us
    dot_general x32, matrix products, add_one(): partial_value = jnp.dot(columns, tile, preferred_element_type=jnp.float32)  49.4 us
    psum x4, blocking collectives, over_axes(): return functools.reduce(lax.psum, axes, shard)  36.1 us
  transfers between devices with their start and end apart: 1, of which 1 were waited for; matrix products, arithmetic and copies ran while one was open for 0% of the time, Pallas kernels for 0%

profile of v1, /device:TPU:1, one launch (start us, length us, event | category | flops | bytes accessed | tf_op | source)
XLA Modules:
  0.0 1042.5 jit_solution(18056465051665482674)
XLA Ops:
  0.6 1.6 copy.23
  4.5 3.0 broadcast_in_dim.49
  7.8 6.6 pad_maximum_fusion
  14.4 203.0 %all_to_all.16 = bf16[32,96,1408]{2,1,0:T(8,128)(2,1)S(1)} all-to-all(bf16[32,96,1408]{2,1,0:T(8,128)(2,1)} %pad_maximum_fusion), channel_id=1, replica_groups=mesh['expert_0'=4,'expert_1'=2,'shard_0'=8,'shard_1'=4] {'shard_0','shar..., dimensions={0} | all-to-all | bytes 17301504 | tf_op jit(solution)/shard_map/all_to_all | solution.py:18
  217.4 5.3 fusion.9
  222.6 9.3 psum.28
  232.0 7.1 psum.29
  239.1 12.3 %psum.30 = f32[]{:T(128)} all-reduce(f32[]{:T(128)} %psum.29), channel_id=1, replica_groups=mesh['expert_0'=4,'expert_1'=2,'shard_0'=8,'shard_1'=4] {'shard_0'}, use_global_device_ids=true, to_apply=%region_4.5 | all-reduce | flops 1 | bytes 8 | tf_op jit(solution)/shard_map/psum | solution.py:29
  251.4 7.4 psum.31
  259.5 5.8 multiply_reduce_fusion
  266.7 13.2 %all_to_all.17 = f32[32,1,2]{2,1,0:T(1,128)S(1)} all-to-all(f32[32,1,2]{2,1,0:T(1,128)S(1)} %broadcast_in_dim.50), channel_id=1, replica_groups=mesh['expert_0'=4,'expert_1'=2,'shard_0'=8,'shard_1'=4] {'shard_0','shar..., dimensions={0} | all-to-all | bytes 512 | tf_op jit(solution)/shard_map/all_to_all | solution.py:34
  282.0 3.0 fusion.14
  285.0 10.2 stack.3
  295.2 5.5 all-to-all-start.2
  300.7 689.7 %all-to-all-done.2 = bf16[32,1,512,896]{3,2,1,0:T(8,128)(2,1)} async-done(((bf16[32,1,512,896]{3,2,1,0:T(8,128)(2,1)}), bf16[32,1,512,896]{3,2,1,0:T(8,128)(2,1)}, u32[]{:S(2)}, u32[]{:S(2)}) %all-to-all-start.2) | async-done | bytes 29360160 | tf_op jit(solution)/shard_map/all_to_all | solution.py:103
  990.6 50.7 %while.15 = (s32[]{:T(128)}, f32[96,7168]{1,0:T(8,128)S(1)}, bf16[96,2048]{1,0:T(8,128)(2,1)}, bf16[32,512,896]{2,1,0:T(8,128)(2,1)}, s32[]{:T(128)}, /*index=5*...) while((s32[]{:T(128)}, f32[96,7168]{1,0:T(8,128)S(1)}, ...), condition=%wide.region_9.10_spmd, body=%wide.region_8.9_spmd.sunk | while | flops 88166424 | bytes 1704796 | solution.py:115
  1001.7 1.5 fusion.23
  1008.1 1.5 fusion.23
  1014.4 1.5 fusion.23
  1020.7 1.5 fusion.23
  1023.9 1.5 fusion.23
  1027.1 1.5 fusion.23
  1033.4 1.5 fusion.23
  1039.7 1.5 fusion.23
  (42 shorter events, 42.6 us)
Async XLA Ops:
  3.2 1.0 copy-start.2
  217.4 42.1 %copy-start = (f32[1,1,512,896]{3,2,1,0:T(8,128)S(1)}, f32[1,1,512,896]{3,2,1,0:T(8,128)}, u32[]{:S(2)}) copy-start(f32[1,1,512,896]{3,2,1,0:T(8,128)} %param.13) | copy-start | bytes 5505028
  217.4 42.1 %copy-start.1 = (bf16[1,1,512,896]{3,2,1,0:T(8,128)(2,1)S(1)}, bf16[1,1,512,896]{3,2,1,0:T(8,128)(2,1)}, u32[]{:S(2)}) copy-start(bf16[1,1,512,896]{3,2,1,0:T(8,128)(2,1)} %param.15) | copy-start | bytes 2752516
  295.2 695.2 %all-to-all-start.2 = ((bf16[32,1,512,896]{3,2,1,0:T(8,128)(2,1)}), bf16[32,1,512,896]{3,2,1,0:T(8,128)(2,1)}, u32[]{:S(2)}, u32[]{:S(2)}) async-start(bf16[32,1,512,896]{3,2,1,0:T(8,128)(2,1)} %stack.3), calls=%async_computation.2 | async-start | bytes 58720256 | tf_op jit(solution)/shard_map/all_to_all | solution.py:103
